TPU v7x, 256 devices: a whole 4x4x8 slice. The times are simulated.
256 devices in a mesh: section: 8 (over z), dp: 32 (over y, x, core).
Axes of the slice: x: 4, y: 4, z: 8, core: 2. Of those that a mesh axis runs over, the one named last changes fastest.
Arguments:
- section_inputs: bfloat16 [8, 8192, 896], P('section', 'dp'), may hold values from -44 to 44
- cotangent: bfloat16 [8192, 896], P('dp'), may hold values from -6 to 6
- norm_gain: float32 [8, 896], P('section'), may hold values from 0.25 to 1.75
- quant_gate: bfloat16 [8, 896, 2432], P('section', 'dp'), may hold values from -1 to 1
- quant_up: bfloat16 [8, 896, 2432], P('section', 'dp'), may hold values from -1 to 1
- scales: float32 [8, 2], P('section'), may hold values from 0.04 to 0.08
- down_proj: bfloat16 [8, 2432, 896], P('section'), may hold values from -0.125 to 0.125
- master_gate: float32 [8, 896, 2432], P('section', 'dp'), may hold values from -0.3 to 0.3
- master_up: float32 [8, 896, 2432], P('section', 'dp'), may hold values from -0.3 to 0.3
- moment_gate: float32 [8, 896, 2432], P('section', 'dp'), may hold values from -3 to 3
- moment_up: float32 [8, 896, 2432], P('section', 'dp'), may hold values from -3 to 3
- second_gate: float32 [8, 896, 2432], P('section', 'dp'), may hold values from 0.05 to 1
- second_up: float32 [8, 896, 2432], P('section', 'dp'), may hold values from 0.05 to 1
- next_inputs: bfloat16 [8, 8192, 896], P('section', 'dp'), may hold values from -44 to 44
Outputs:
- input_grads: bfloat16 [8, 8192, 896], P('section', 'dp')
- master_gate_new: float32 [8, 896, 2432], P('section', 'dp')
- master_up_new: float32 [8, 896, 2432], P('section', 'dp')
- moment_gate_new: float32 [8, 896, 2432], P('section', 'dp')
- moment_up_new: float32 [8, 896, 2432], P('section', 'dp')
- second_gate_new: float32 [8, 896, 2432], P('section', 'dp')
- second_up_new: float32 [8, 896, 2432], P('section', 'dp')
- new_scales: float32 [8, 2], P('section')
- next_hidden: bfloat16 [8, 8192, 2432], P('section', 'dp')
All inputs are finite; a program needn't handle non-finite values. Where the computation divides by a largest or mean magnitude, that divisor is 1e-20 or more.
Results may differ from a plain program's by a relative error of at most 0.034.
Values may be sent and summed in bfloat16 or wider, within the bound.
A program may use at most 128 MiB of HBM per device.

v0:
```python
import jax
import jax.numpy as jnp
from jax import lax
from jax.sharding import PartitionSpec as P

beta_one = 0.9
beta_two = 0.95
learn_rate = 0.002
decay_rate = 0.1
adam_steps = 100.0
norm_eps = 1e-06
adam_eps = 1e-08
scale_eps = 1e-06


def shifted(value, axis, steps):
    count = lax.axis_size(axis)
    first, last = (max(0, -steps), min(count, count - steps))
    return lax.ppermute(value, axis, [(source, source + steps) for source in range(first, last)])


def normalize(inputs, norm_gain):
    widened = inputs.astype(jnp.float32)
    inverse = lax.rsqrt(jnp.mean(widened * widened, axis=-1, keepdims=True) + norm_eps)
    return (widened, inverse, (widened * inverse * norm_gain).astype(jnp.bfloat16))


def silu_slope(preact):
    sigmoid = jax.nn.sigmoid(preact)
    return (preact * sigmoid, sigmoid * (1.0 + preact * (1.0 - sigmoid)))


def transposed(first_op, second_op):
    return lax.dot_general(
        first_op, second_op, (((1,), (1,)), ((), ())), preferred_element_type=jnp.float32
    )


def block_back(
    widened, inverse, normed, norm_gain, gate_full, up_full, scale_pair, down_full, upstream
):
    gate_pre = jnp.dot(normed, gate_full, preferred_element_type=jnp.float32) * scale_pair[0]
    up_pre = jnp.dot(normed, up_full, preferred_element_type=jnp.float32) * scale_pair[1]
    hidden_grad = transposed(upstream, down_full)
    active, slopes = silu_slope(gate_pre)
    gate_grad = (hidden_grad * up_pre * slopes).astype(jnp.bfloat16)
    up_grad = (hidden_grad * active).astype(jnp.bfloat16)
    normed_grad = (
        transposed(gate_grad, gate_full) * scale_pair[0]
        + transposed(up_grad, up_full) * scale_pair[1]
    )
    gained = norm_gain * normed_grad
    mean_term = jnp.mean(widened * gained, axis=-1, keepdims=True)
    result = (
        upstream.astype(jnp.float32)
        + inverse * gained
        - widened * (inverse * inverse * inverse) * mean_term
    )
    return (result.astype(jnp.bfloat16), jnp.concatenate([gate_grad, up_grad], axis=1))


def adam_update(master, moment_old, second_old, gradient):
    moment_one = beta_one * moment_old + (1.0 - beta_one) * gradient
    moment_two = beta_two * second_old + (1.0 - beta_two) * gradient * gradient
    unbiased_one = moment_one / (1.0 - beta_one**adam_steps)
    unbiased_two = moment_two / (1.0 - beta_two**adam_steps)
    updated = master - learn_rate * (
        unbiased_one / (jnp.sqrt(unbiased_two) + adam_eps) + decay_rate * master
    )
    return (updated, moment_one, moment_two)


def shards(
    section_inputs,
    cotangent,
    norm_gain,
    quant_gate,
    quant_up,
    scales,
    down_proj,
    master_gate,
    master_up,
    moment_gate,
    moment_up,
    second_gate,
    second_up,
    next_inputs,
):
    gain_row = norm_gain[0]
    scale_pair = scales[0]
    down_local = down_proj[0]
    tok_rows = section_inputs.shape[1]
    feature_count = section_inputs.shape[2]
    hidden_count = quant_gate.shape[2]
    sections = lax.axis_size("section")
    position = lax.axis_index("section")
    gate_full, up_full = (
        lax.all_gather(quant_gate[0], "dp", axis=0, tiled=True),
        lax.all_gather(quant_up[0], "dp", axis=0, tiled=True),
    )
    widened, inverse, normed = normalize(section_inputs[0], gain_row)
    blocks = tok_rows // tok_rows
    turn_count = sections + blocks - 1
    last_section = sections - 1

    def one_turn(turn_index, loop_state):
        incoming, grads_all, result_all = loop_state
        micro_index = turn_index - (last_section - position)
        is_active = jnp.logical_and(micro_index >= 0, micro_index < blocks)
        upstream = jnp.where(position == last_section, cotangent, incoming)

        def working(buffers):
            result, grads_both = block_back(
                widened,
                inverse,
                normed,
                gain_row,
                gate_full,
                up_full,
                scale_pair,
                down_local,
                upstream,
            )
            return (result, (grads_both, result))

        def resting(buffers):
            return (jnp.zeros((tok_rows, feature_count), jnp.bfloat16), buffers)

        outgoing, stored = lax.cond(is_active, working, resting, (grads_all, result_all))
        incoming = shifted(outgoing, "section", -1)
        return (incoming, stored[0], stored[1])

    start_state = (
        jnp.zeros((tok_rows, feature_count), jnp.bfloat16),
        jnp.zeros((tok_rows, 2 * hidden_count), jnp.bfloat16),
        jnp.zeros((tok_rows, feature_count), jnp.bfloat16),
    )
    incoming, grads_all, result_all = lax.fori_loop(0, turn_count, one_turn, start_state)
    columns = normed
    summed = lax.psum_scatter(
        lax.dot_general(
            columns, grads_all, (((0,), (0,)), ((), ())), preferred_element_type=jnp.float32
        ).astype(jnp.bfloat16),
        "dp",
        scatter_dimension=0,
        tiled=True,
    ).astype(jnp.float32)
    new_gate, mom_gate, sec_gate = adam_update(
        master_gate[0], moment_gate[0], second_gate[0], summed[:, :hidden_count]
    )
    new_up, mom_up, sec_up = adam_update(
        master_up[0], moment_up[0], second_up[0], summed[:, hidden_count:]
    )
    peak_pair = lax.pmax((jnp.max(jnp.abs(new_gate)), jnp.max(jnp.abs(new_up))), "dp")
    scale_gate = peak_pair[0] + scale_eps
    scale_up = peak_pair[1] + scale_eps
    quant_next_gate = (new_gate / scale_gate).astype(jnp.bfloat16)
    quant_next_up = (new_up / scale_up).astype(jnp.bfloat16)
    unused_one, unused_two, next_normed = normalize(next_inputs[0], gain_row)
    stacked = jnp.concatenate([quant_next_gate, quant_next_up], axis=1)
    columns = next_normed
    gathered_sum = jnp.dot(
        columns,
        lax.all_gather(stacked, "dp", axis=0, tiled=True),
        preferred_element_type=jnp.float32,
    )
    gate_next = gathered_sum[:, :hidden_count] * scale_gate
    up_next = gathered_sum[:, hidden_count:] * scale_up
    next_hidden = (jax.nn.silu(gate_next) * up_next).astype(jnp.bfloat16)
    return (
        result_all[None],
        new_gate[None],
        new_up[None],
        mom_gate[None],
        mom_up[None],
        sec_gate[None],
        sec_up[None],
        jnp.stack([scale_gate, scale_up])[None, :],
        next_hidden[None],
    )


def solution(mesh):
    placed = (
        P("section", "dp", None),
        P("dp", None),
        P("section", None),
        P("section", "dp", None),
        P("section", "dp", None),
        P("section", None),
        P("section", None, None),
        P("section", "dp", None),
        P("section", "dp", None),
        P("section", "dp", None),
        P("section", "dp", None),
        P("section", "dp", None),
        P("section", "dp", None),
        P("section", "dp", None),
    )
    return jax.shard_map(
        shards,
        mesh=mesh,
        in_specs=placed,
        out_specs=(
            P("section", "dp", None),
            P("section", "dp", None),
            P("section", "dp", None),
            P("section", "dp", None),
            P("section", "dp", None),
            P("section", "dp", None),
            P("section", "dp", None),
            P("section", None),
            P("section", "dp", None),
        ),
        check_vma=False,
    )
```

profile of v0, /device:TPU:1, one launch (start us, length us, event | category | flops | bytes accessed | tf_op | source)
XLA Modules:
  0.0 663.7 jit_solution(10555207298454545981)
XLA Ops:
  14.3 59.9 %all-gather.9.cloned.1.call-done = bf16[1,896,2432]{2,0,1:T(2,128)(2,1)} async-done(((bf16[1,28,2432]{2,0,1:T(2,128)(2,1)}), bf16[1,896,2432]{2,0,1:T(2,128)(2,1)}) %all-gather.9.cloned.1.call-update) | async-done | bytes 4358160 | tf_op jit(solution)/shard_map/all_gather | solution.py:98
  74.2 6.1 copy.123
  80.3 55.4 %all-gather.7.cloned.1.call-done = bf16[1,896,2432]{2,0,1:T(2,128)(2,1)} async-done(((bf16[1,28,2432]{2,0,1:T(2,128)(2,1)}), bf16[1,896,2432]{2,0,1:T(2,128)(2,1)}) %all-gather.7.cloned.1.call-update) | async-done | bytes 4358160 | tf_op jit(solution)/shard_map/all_gather | solution.py:99
  135.7 6.2 copy.124
  143.6 238.6 %while.19 = (s32[]{:T(128)}, bf16[256,896]{1,0:T(8,128)(2,1)S(1)}, bf16[256,4864]{1,0:T(8,128)(2,1)}, bf16[256,896]{1,0:T(8,128)(2,1)S(1)}, s32[]{:T(128)}, /*in...) while((s32[]{:T(128)}, bf16[256,896]{1,0:T(8,128)(2,1)S(1)}, ...), condition=%wide.region_5.6_spmd, body=%wide.region_1.5_spmd.sunk | while | flops 5598052864 | bytes 99273736 | solution.py:138
  145.7 12.7 %collective-permute-done = bf16[256,896]{1,0:T(8,128)(2,1)S(1)} collective-permute-done((bf16[256,896]{1,0:T(8,128)(2,1)}, bf16[256,896]{1,0:T(8,128)(2,1)S(1)}, u32[]{:S(2)}, u32[]{:S(2)}) %collective-permute-start) | collective-permute-done | bytes 458784 | tf_op jit(solution)/shard_map/while/body/eval_jaxpr/ppermute | solution.py:19
  160.5 11.8 %collective-permute-done = bf16[256,896]{1,0:T(8,128)(2,1)S(1)} collective-permute-done((bf16[256,896]{1,0:T(8,128)(2,1)}, bf16[256,896]{1,0:T(8,128)(2,1)S(1)}, u32[]{:S(2)}, u32[]{:S(2)}) %collective-permute-start) | collective-permute-done | bytes 458784 | tf_op jit(solution)/shard_map/while/body/eval_jaxpr/ppermute | solution.py:19
  174.4 10.8 %collective-permute-done = bf16[256,896]{1,0:T(8,128)(2,1)S(1)} collective-permute-done((bf16[256,896]{1,0:T(8,128)(2,1)}, bf16[256,896]{1,0:T(8,128)(2,1)S(1)}, u32[]{:S(2)}, u32[]{:S(2)}) %collective-permute-start) | collective-permute-done | bytes 458784 | tf_op jit(solution)/shard_map/while/body/eval_jaxpr/ppermute | solution.py:19
  187.3 12.4 %collective-permute-done = bf16[256,896]{1,0:T(8,128)(2,1)S(1)} collective-permute-done((bf16[256,896]{1,0:T(8,128)(2,1)}, bf16[256,896]{1,0:T(8,128)(2,1)S(1)}, u32[]{:S(2)}, u32[]{:S(2)}) %collective-permute-start) | collective-permute-done | bytes 458784 | tf_op jit(solution)/shard_map/while/body/eval_jaxpr/ppermute | solution.py:19
  201.7 10.1 %collective-permute-done = bf16[256,896]{1,0:T(8,128)(2,1)S(1)} collective-permute-done((bf16[256,896]{1,0:T(8,128)(2,1)}, bf16[256,896]{1,0:T(8,128)(2,1)S(1)}, u32[]{:S(2)}, u32[]{:S(2)}) %collective-permute-start) | collective-permute-done | bytes 458784 | tf_op jit(solution)/shard_map/while/body/eval_jaxpr/ppermute | solution.py:19
  213.9 9.3 %collective-permute-done = bf16[256,896]{1,0:T(8,128)(2,1)S(1)} collective-permute-done((bf16[256,896]{1,0:T(8,128)(2,1)}, bf16[256,896]{1,0:T(8,128)(2,1)S(1)}, u32[]{:S(2)}, u32[]{:S(2)}) %collective-permute-start) | collective-permute-done | bytes 458784 | tf_op jit(solution)/shard_map/while/body/eval_jaxpr/ppermute | solution.py:19
  225.3 129.3 %collective-permute-done = bf16[256,896]{1,0:T(8,128)(2,1)S(1)} collective-permute-done((bf16[256,896]{1,0:T(8,128)(2,1)}, bf16[256,896]{1,0:T(8,128)(2,1)S(1)}, u32[]{:S(2)}, u32[]{:S(2)}) %collective-permute-start) | collective-permute-done | bytes 458784 | tf_op jit(solution)/shard_map/while/body/eval_jaxpr/ppermute | solution.py:19
  354.6 18.2 %conditional.2 = (bf16[256,896]{1,0:T(8,128)(2,1)}, bf16[256,4864]{1,0:T(8,128)(2,1)}, bf16[256,896]{1,0:T(8,128)(2,1)S(1)}) conditional(s32[]{:T(128)} %convert_element_type.82, (bf16[256,4864]{1,0:T(8,128)(2,1)}, bf16[256,896]{1,0:T(8,128)(2,1)S(1)}) %tuple.67, (pred[]{:T(512)}, bf16[256,896]{1,0:T(8,128)(2,1)S(1)}, bf16[256,896]{1,0:T(8,128)(2,1)S(1)}, ...), branch_computations={%region_2.2_spmd, %region_3.4_spmd} | conditional | flops 5598052864 | bytes 97438392 | solution.py:129
  355.2 4.9 convolution_multiply_fusion
  374.1 8.1 %collective-permute-done = bf16[256,896]{1,0:T(8,128)(2,1)S(1)} collective-permute-done((bf16[256,896]{1,0:T(8,128)(2,1)}, bf16[256,896]{1,0:T(8,128)(2,1)S(1)}, u32[]{:S(2)}, u32[]{:S(2)}) %collective-permute-start) | collective-permute-done | bytes 458784 | tf_op jit(solution)/shard_map/while/body/eval_jaxpr/ppermute | solution.py:19
  382.2 7.7 %convolution_convert_fusion = bf16[896,4864]{1,0:T(8,128)(2,1)} fusion(bf16[256,896]{1,0:T(8,128)(2,1)S(1)} %get-tuple-element.638, bf16[256,4864]{1,0:T(8,128)(2,1)} %get-tuple-element.385), kind=kOutput, calls=%fused_computation.18 | convolution fusion | flops 2235727872 | bytes 11665408 | tf_op jit(solution)/shard_map/dot_general | solution.py:141
  390.0 92.3 %fusion = bf16[32,4864]{1,0:T(8,128)(2,1)S(1)} fusion(bf16[896,4864]{1,0:T(8,128)(2,1)} %convolution_convert_fusion), kind=kCustom, calls=%all-reduce-scatter | all-reduce-scatter fusion | flops 4980737 | bytes 9028608
  487.6 2.7 collective-permute-start.4
  491.6 14.2 %collective-permute-done.4 = bf16[28,4864]{1,0:T(8,128)(2,1)S(1)} collective-permute-done((bf16[28,4864]{1,0:T(8,128)(2,1)S(1)}, bf16[28,4864]{1,0:T(8,128)(2,1)S(1)}, u32[]{:S(2)}, u32[]{:S(2)}) %collective-permute-start.4) | collective-permute-done | bytes 272416
  505.8 8.6 %concatenate.7 = bf16[156,4864]{1,0:T(8,128)(2,1)S(1)} concatenate(bf16[28,4864]{1,0:T(8,128)(2,1)S(1)} %collective-permute-done.4, bf16[32,4864]{1,0:T(8,128)(2,1)S(1)} %collective-permute-done.3, bf16[32,4864]{1,0:T(8,128)(2,1)S(1)} %collective-permute-done.2, bf16[32,4864]{1,0:T(8,128)(2,1)S(1)} %collective-permute-done.1, bf16[32,4864]{1,0:T(8,128)(2,1)S(1)} %fusion), dimensions={0} | concatenate | bytes 3035136
  517.0 64.8 %all-reduce.2 = (f32[]{:T(128)}, f32[]{:T(128)}) all-reduce(f32[]{:T(128)} %get-tuple-element.470, f32[]{:T(128)} %get-tuple-element.454), channel_id=1, replica_groups=mesh['section'=8,'dp'=32] {'dp'}, use_global_device_ids=true, to_apply=%region_10.11 | all-reduce | flops 2 | bytes 16 | tf_op jit(solution)/shard_map/pmax | solution.py:154
  590.7 46.3 %all-gather.11.cloned.1.call-done = bf16[32,28,4864]{2,1,0:T(8,128)(2,1)} async-done(((bf16[1,28,4864]{2,1,0:T(8,128)(2,1)}), bf16[32,28,4864]{2,1,0:T(8,128)(2,1)}) %all-gather.11.cloned.1.call-update) | async-done | bytes 8716304 | tf_op jit(solution)/shard_map/all_gather | solution.py:164
  637.0 12.9 %reshape.68 = bf16[896,4864]{1,0:T(8,128)(2,1)} reshape(bf16[32,28,4864]{2,1,0:T(8,128)(2,1)} %all-gather.11.cloned.1.call-done) | data formatting | bytes 17432576
  649.9 5.5 fusion.13
  (99 shorter events, 61.0 us)
Async XLA Ops:
  7.2 7.0 %copy-start.1 = (bf16[1,256,896]{2,1,0:T(8,128)(2,1)S(1)}, bf16[1,256,896]{2,1,0:T(8,128)(2,1)}, u32[]{:S(2)}) copy-start(bf16[1,256,896]{2,1,0:T(8,128)(2,1)} %param.18) | copy-start | bytes 1376260
  7.2 67.0 %all-gather.9.cloned.1.call-start = ((), (), s32[]{:S(2)}) async-start(), calls=%async_computation.1 | async-start | bytes 8988672 | tf_op jit(solution)/shard_map/all_gather | solution.py:98
  9.1 126.6 %all-gather.7.cloned.1.call-start = ((), (), s32[]{:S(2)}) async-start(), calls=%async_computation | async-start | bytes 8988672 | tf_op jit(solution)/shard_map/all_gather | solution.py:99
  11.0 626.0 %all-gather.11.cloned.1.call-start = ((), (), s32[]{:S(2)}) async-start(), calls=%async_computation.2 | async-start | bytes 10272768 | tf_op jit(solution)/shard_map/all_gather | solution.py:164
  144.4 14.0 %collective-permute-start = (bf16[256,896]{1,0:T(8,128)(2,1)}, bf16[256,896]{1,0:T(8,128)(2,1)S(1)}, u32[]{:S(2)}, u32[]{:S(2)}) collective-permute-start(bf16[256,896]{1,0:T(8,128)(2,1)} %get-tuple-element.568), channel_id=1, source_target_pairs={{32,0},{64,32},{96,64},{128,96},{160,128},{192,160},{224,192},{33,... | collective-permute-start | bytes 1376264 | tf_op jit(solution)/shard_map/while/body/eval_jaxpr/ppermute | solution.py:19
  159.2 13.0 %collective-permute-start = (bf16[256,896]{1,0:T(8,128)(2,1)}, bf16[256,896]{1,0:T(8,128)(2,1)S(1)}, u32[]{:S(2)}, u32[]{:S(2)}) collective-permute-start(bf16[256,896]{1,0:T(8,128)(2,1)} %get-tuple-element.568), channel_id=1, source_target_pairs={{32,0},{64,32},{96,64},{128,96},{160,128},{192,160},{224,192},{33,... | collective-permute-start | bytes 1376264 | tf_op jit(solution)/shard_map/while/body/eval_jaxpr/ppermute | solution.py:19
  173.1 12.1 %collective-permute-start = (bf16[256,896]{1,0:T(8,128)(2,1)}, bf16[256,896]{1,0:T(8,128)(2,1)S(1)}, u32[]{:S(2)}, u32[]{:S(2)}) collective-permute-start(bf16[256,896]{1,0:T(8,128)(2,1)} %get-tuple-element.568), channel_id=1, source_target_pairs={{32,0},{64,32},{96,64},{128,96},{160,128},{192,160},{224,192},{33,... | collective-permute-start | bytes 1376264 | tf_op jit(solution)/shard_map/while/body/eval_jaxpr/ppermute | solution.py:19
  186.0 13.7 %collective-permute-start = (bf16[256,896]{1,0:T(8,128)(2,1)}, bf16[256,896]{1,0:T(8,128)(2,1)S(1)}, u32[]{:S(2)}, u32[]{:S(2)}) collective-permute-start(bf16[256,896]{1,0:T(8,128)(2,1)} %get-tuple-element.568), channel_id=1, source_target_pairs={{32,0},{64,32},{96,64},{128,96},{160,128},{192,160},{224,192},{33,... | collective-permute-start | bytes 1376264 | tf_op jit(solution)/shard_map/while/body/eval_jaxpr/ppermute | solution.py:19
  200.5 11.4 %collective-permute-start = (bf16[256,896]{1,0:T(8,128)(2,1)}, bf16[256,896]{1,0:T(8,128)(2,1)S(1)}, u32[]{:S(2)}, u32[]{:S(2)}) collective-permute-start(bf16[256,896]{1,0:T(8,128)(2,1)} %get-tuple-element.568), channel_id=1, source_target_pairs={{32,0},{64,32},{96,64},{128,96},{160,128},{192,160},{224,192},{33,... | collective-permute-start | bytes 1376264 | tf_op jit(solution)/shard_map/while/body/eval_jaxpr/ppermute | solution.py:19
  212.6 10.6 %collective-permute-start = (bf16[256,896]{1,0:T(8,128)(2,1)}, bf16[256,896]{1,0:T(8,128)(2,1)S(1)}, u32[]{:S(2)}, u32[]{:S(2)}) collective-permute-start(bf16[256,896]{1,0:T(8,128)(2,1)} %get-tuple-element.568), channel_id=1, source_target_pairs={{32,0},{64,32},{96,64},{128,96},{160,128},{192,160},{224,192},{33,... | collective-permute-start | bytes 1376264 | tf_op jit(solution)/shard_map/while/body/eval_jaxpr/ppermute | solution.py:19
  224.0 130.6 %collective-permute-start = (bf16[256,896]{1,0:T(8,128)(2,1)}, bf16[256,896]{1,0:T(8,128)(2,1)S(1)}, u32[]{:S(2)}, u32[]{:S(2)}) collective-permute-start(bf16[256,896]{1,0:T(8,128)(2,1)} %get-tuple-element.568), channel_id=1, source_target_pairs={{32,0},{64,32},{96,64},{128,96},{160,128},{192,160},{224,192},{33,... | collective-permute-start | bytes 1376264 | tf_op jit(solution)/shard_map/while/body/eval_jaxpr/ppermute | solution.py:19
  355.2 5.0 copy-start.8
  355.2 6.7 %slice-start.2 = ((s8[4358144]{0:T(1024)(128)(4,1)}), s8[4194304]{0:T(1024)(128)(4,1)S(1)}, s32[]{:S(2)}) async-start(s8[4358144]{0:T(1024)(128)(4,1)} %bitcast.111), calls=%async_computation.5 | async-start | bytes 8388608 | tf_op jit(solution)/shard_map/while/body/eval_jaxpr/cond
  360.2 6.5 slice-start
  362.0 4.8 slice-start.1
  372.8 9.4 %collective-permute-start = (bf16[256,896]{1,0:T(8,128)(2,1)}, bf16[256,896]{1,0:T(8,128)(2,1)S(1)}, u32[]{:S(2)}, u32[]{:S(2)}) collective-permute-start(bf16[256,896]{1,0:T(8,128)(2,1)} %get-tuple-element.568), channel_id=1, source_target_pairs={{32,0},{64,32},{96,64},{128,96},{160,128},{192,160},{224,192},{33,... | collective-permute-start | bytes 1376264 | tf_op jit(solution)/shard_map/while/body/eval_jaxpr/ppermute | solution.py:19
  382.2 7.7 %copy-start.3 = (bf16[256,896]{1,0:T(8,128)(2,1)}, bf16[256,896]{1,0:T(8,128)(2,1)S(1)}, u32[]{:S(2)}) copy-start(bf16[256,896]{1,0:T(8,128)(2,1)S(1)} %get-tuple-element.384) | copy-start | bytes 1376260
  390.0 100.4 %copy-start.7 = (u32[256]{0:T(256)S(1)}, u32[256]{0:T(256)}, u32[]{:S(2)}) copy-start(u32[256]{0:T(256)} %constant.99) | copy-start | bytes 3076
  482.2 32.3 %copy-start.4 = (f32[1,28,2432]{2,0,1:T(1,128)S(1)}, f32[1,28,2432]{2,0,1:T(1,128)}, u32[]{:S(2)}) copy-start(f32[1,28,2432]{2,0,1:T(1,128)} %param.29) | copy-start | bytes 817156
  482.3 23.5 %collective-permute-start.3 = (bf16[32,4864]{1,0:T(8,128)(2,1)S(1)}, bf16[32,4864]{1,0:T(8,128)(2,1)S(1)}, u32[]{:S(2)}, u32[]{:S(2)}) collective-permute-start(bf16[32,4864]{1,0:T(8,128)(2,1)S(1)} %fusion), channel_id=1, source_target_pairs={{0,3},{1,4},{2,5},{3,6},{4,7},{5,8},{6,9},{7,10},{8,11},{9,12},{10... | collective-permute-start | bytes 933896
  483.9 21.9 %collective-permute-start.2 = (bf16[32,4864]{1,0:T(8,128)(2,1)S(1)}, bf16[32,4864]{1,0:T(8,128)(2,1)S(1)}, u32[]{:S(2)}, u32[]{:S(2)}) collective-permute-start(bf16[32,4864]{1,0:T(8,128)(2,1)S(1)} %fusion), channel_id=1, source_target_pairs={{0,2},{1,3},{2,4},{3,5},{4,6},{5,7},{6,8},{7,9},{8,10},{9,11},{10,... | collective-permute-start | bytes 933896
  485.2 20.6 %collective-permute-start.1 = (bf16[32,4864]{1,0:T(8,128)(2,1)S(1)}, bf16[32,4864]{1,0:T(8,128)(2,1)S(1)}, u32[]{:S(2)}, u32[]{:S(2)}) collective-permute-start(bf16[32,4864]{1,0:T(8,128)(2,1)S(1)} %fusion), channel_id=1, source_target_pairs={{0,1},{1,2},{2,3},{3,4},{4,5},{5,6},{6,7},{7,8},{8,9},{9,10},{10,1... | collective-permute-start | bytes 933896
  487.6 18.1 %collective-permute-start.4 = (bf16[28,4864]{1,0:T(8,128)(2,1)S(1)}, bf16[28,4864]{1,0:T(8,128)(2,1)S(1)}, u32[]{:S(2)}, u32[]{:S(2)}) collective-permute-start(bf16[28,4864]{1,0:T(8,128)(2,1)S(1)} %slice.28), channel_id=1, source_target_pairs={{0,4},{1,5},{2,6},{3,7},{4,8},{5,9},{6,10},{7,11},{8,12},{9,13},{1... | collective-permute-start | bytes 817160
  514.5 69.5 %copy-start.2 = (bf16[1,256,896]{2,1,0:T(8,128)(2,1)S(1)}, bf16[1,256,896]{2,1,0:T(8,128)(2,1)}, u32[]{:S(2)}) copy-start(bf16[1,256,896]{2,1,0:T(8,128)(2,1)} %param.31) | copy-start | bytes 1376260
  (4 other events, 6.8 us)
Sparse Core Ops, SparseCore 0:
  11.2 62.9 all-gather.8
  77.4 58.3 all-gather.6
  584.1 52.8 all-gather.10
where the time goes:
time: 665 us; the launch traced here: 664 us
  waiting for transfers between devices  380 us (57%)
  blocking collectives  157 us (24%)
  local copies, waits for them, and re-layouts  53.1 us (8%)
  matrix products  27 us (4%)
  starting transfers between devices  18.3 us (3%)
  between operations  15.9 us (2%)
  other arithmetic  11.7 us (2%)
    ppermute x8, waiting for transfers between devices, shifted(): lax.ppermute(value, axis, [(source, source + steps) for source in range(f...  204 us
    unnamed x1, blocking collectives  92.3 us
    pmax x1, blocking collectives, shards(): lax.pmax((jnp.max(jnp.abs(new_gate)), jnp.max(jnp.abs(new_up))), 'dp')  64.8 us
    all_gather x1, waiting for transfers between devices, shards(): lax.all_gather(quant_gate[0], 'dp', axis=0, tiled=True)  59.9 us
    all_gather x1, waiting for transfers between devices, shards(): lax.all_gather(quant_up[0], 'dp', axis=0, tiled=True)  55.4 us
    all_gather x1, waiting for transfers between devices, shards(): lax.all_gather(stacked, 'dp', axis=0, tiled=True)  46.3 us
    unnamed x30, local copies, waits for them, and re-layouts  44.2 us
    unnamed x7, waiting for transfers between devices  14.3 us
  transfers between devices with their start and end apart: 15, of which 12 were waited for; matrix products, arithmetic and copies ran while one was open for 3% of the time, Pallas kernels for 0%

commit v1 on v0

v1 whole, which is shorter than its diff:
```python
import functools
import jax
import jax.numpy as jnp
from jax import lax
from jax.experimental import pallas as pl
from jax.experimental.pallas import tpu as pltpu
from jax.sharding import PartitionSpec as P

beta_one = 0.9
beta_two = 0.95
learn_rate = 0.002
decay_rate = 0.1
adam_steps = 100.0
norm_eps = 1e-06
adam_eps = 1e-08
scale_eps = 1e-06

RING = 4
CORES = 2
ROWS = 28
PAD = 32
MICRO = 4
F32 = jnp.float32
BF16 = jnp.bfloat16
NT = (((1,), (1,)), ((), ()))
NN = (((1,), (0,)), ((), ()))


def mm(a, b, dims=NN):
    return lax.dot_general(a, b, dims, preferred_element_type=F32)


def tiles(count, step=512):
    return [(i, min(step, count - i)) for i in range(0, count, step)]


def coords():
    dp = lax.axis_index("dp")
    chip = dp // CORES
    return chip // RING, chip % RING, dp % CORES


def dp_index(y, x, core):
    return (y * RING + x) * CORES + core


class Copies:
    def __init__(self, send_sem, recv_sem):
        self.send_sem, self.recv_sem = send_sem, recv_sem
        self.sent = []
        self.slots = {}

    def slot(self, key):
        return self.slots.setdefault(key, len(self.slots))

    def start(self, src, dst, key, device):
        copy = pltpu.make_async_remote_copy(
            src_ref=src,
            dst_ref=dst,
            send_sem=self.send_sem.at[len(self.sent)],
            recv_sem=self.recv_sem.at[self.slot(key)],
            device_id={"dp": device},
            device_id_type=pl.DeviceIdType.MESH,
        )
        copy.start()
        self.sent.append(copy)

    def wait_recv(self, dst, key):
        pltpu.make_async_remote_copy(
            src_ref=dst,
            dst_ref=dst,
            send_sem=self.send_sem.at[0],
            recv_sem=self.recv_sem.at[self.slot(key)],
            device_id={"dp": lax.axis_index("dp")},
            device_id_type=pl.DeviceIdType.MESH,
        ).wait_recv()

    def wait_sends(self):
        for copy in self.sent:
            copy.wait_send()


def plane_barrier(extra=()):
    y, x, core = coords()
    sem = pltpu.get_barrier_semaphore()
    for device in (
        dp_index((y + 1) % RING, x, core),
        dp_index((y + RING - 1) % RING, x, core),
        dp_index(y, (x + 1) % RING, core),
        dp_index(y, (x + RING - 1) % RING, core),
        dp_index(y, x, 1 - core),
    ):
        pl.semaphore_signal(sem, inc=1, device_id={"dp": device}, device_id_type=pl.DeviceIdType.MESH)
    for section in extra:
        pl.semaphore_signal(sem, inc=1, device_id={"section": section}, device_id_type=pl.DeviceIdType.MESH)
    pl.semaphore_wait(sem, 5 + len(extra))


def gather_steps(buf, copies, hidden):
    y, x, core = coords()

    def place(half, first, second):
        if half == 0:
            return (y + second) % RING, (x + first) % RING
        return (y + first) % RING, (x + second) % RING

    def piece(half, first, second, which, owner_core=None):
        py, px = place(half, first, second)
        base = dp_index(py, px, core if owner_core is None else owner_core) * PAD
        start, size = {None: (0, PAD), 0: (0, PAD // 2), 1: (PAD // 2, PAD // 2)}[which]
        start = pl.multiple_of(base + start, PAD // 2)
        return buf.at[pl.ds(start, size), pl.ds(half * hidden, hidden)]

    def send(half, first, second, which, axis, step):
        if axis == 0:
            py, px = place(half, step, 0)
            key = ("ag", half, (first - step) % RING, second, which)
        else:
            py, px = place(half, 0, step)
            key = ("ag", half, first, (second - step) % RING, which)
        ref = piece(half, first, second, which)
        copies.start(ref, ref, key, dp_index(py, px, core))

    def sibling(half, first, second):
        ref = piece(half, first, second, None)
        copies.start(ref, ref, ("sib", half, first, second), dp_index(y, x, 1 - core))

    def arrive(half, first, second):
        for which in (0, 1) if 2 in (first if second == 0 else second,) else (None,):
            copies.wait_recv(piece(half, first, second, which), ("ag", half, first, second, which))

    def spread(half, first):
        send(half, first, 0, None, 1, 1)
        send(half, first, 0, None, 1, -1)

    def on_first(half, first):
        arrive(half, first, 0)
        if first == 3:
            send(half, first, 0, 0, 0, 1)
        if first == 1:
            send(half, first, 0, 1, 0, -1)
        spread(half, first)
        sibling(half, first, 0)

    def on_second(half, first, second):
        arrive(half, first, second)
        if second == 3:
            send(half, first, second, 0, 1, 1)
        if second == 1:
            send(half, first, second, 1, 1, -1)
        sibling(half, first, second)

    def begin(half):
        send(half, 0, 0, None, 0, 1)
        send(half, 0, 0, None, 0, -1)
        spread(half, 0)
        sibling(half, 0, 0)

    steps = []
    for first in (3, 1):
        steps += [functools.partial(on_first, half, first) for half in (0, 1)]
    for second in (3, 1):
        steps += [functools.partial(on_second, half, 0, second) for half in (0, 1)]
    steps += [functools.partial(on_first, half, 2) for half in (0, 1)]
    for first in (3, 1, 2):
        for second in (3, 1):
            steps += [functools.partial(on_second, half, first, second) for half in (0, 1)]
    for first in (0, 3, 1, 2):
        steps += [functools.partial(on_second, half, first, 2) for half in (0, 1)]

    def finish():
        for first in (0, 3, 1, 2):
            for second in (0, 3, 1, 2):
                for half in (0, 1):
                    copies.wait_recv(
                        piece(half, first, second, None, 1 - core), ("sib", half, first, second)
                    )

    return begin, steps, finish


def pad_matrix(spread_ref, features):
    padded = spread_ref.shape[1]
    chunk = 128
    for start in range(0, features, chunk):
        row = lax.broadcasted_iota(jnp.int32, (chunk, padded), 0) + start
        col = lax.broadcasted_iota(jnp.int32, (chunk, padded), 1)
        block, inner = col // PAD, col % PAD
        hit = jnp.logical_and(inner < ROWS, block * ROWS + inner == row)
        spread_ref[pl.ds(start, chunk), :] = jnp.where(hit, 1.0, 0.0).astype(BF16)


def rms(inputs):
    widened = inputs.astype(F32)
    return widened, lax.rsqrt(jnp.mean(widened * widened, axis=-1, keepdims=True) + norm_eps)


def back_kernel(
    own_ref, x_ref, cot_ref, gain_ref, scale_ref, down_ref,
    result_ref, rail_ref,
    weights, down_raw, down_pad, spread, normed_pad, wide_pad, inv_ref, gain_pad,
    slope_gate, slope_up, upstream, outgoing, grads, sides,
    send_sem, recv_sem, wave_send, wave_recv, local_sem,
):
    y, x, core = coords()
    section = lax.axis_index("section")
    sections = lax.axis_size("section")
    tokens, features = x_ref.shape
    hidden = down_ref.shape[0]
    padded = spread.shape[1]
    rail = padded // CORES
    chunk = tokens // MICRO
    copies = Copies(send_sem, recv_sem)
    fetch = pltpu.make_async_copy(down_ref, down_raw, local_sem)
    fetch.start()
    mine = pl.multiple_of(lax.axis_index("dp") * PAD, PAD)
    weights[pl.ds(mine, PAD), :] = own_ref[...]
    plane_barrier(((section + 1) % sections, (section + sections - 1) % sections))
    begin, steps, finish = gather_steps(weights, copies, hidden)
    begin(0)
    begin(1)

    pad_matrix(spread, features)
    steps = list(steps)

    def advance(count):
        for _ in range(min(count, len(steps))):
            steps.pop(0)()

    widened, inverse = rms(x_ref[...])
    gain = gain_ref[...]
    normed = (widened * inverse * gain).astype(BF16)
    inv_ref[...] = inverse
    high = gain.astype(BF16)
    rest = gain - high.astype(F32)
    middle = rest.astype(BF16)
    low = (rest - middle.astype(F32)).astype(BF16)
    one_hot = spread[...]
    gain_pad[...] = mm(high, one_hot) + mm(middle, one_hot) + mm(low, one_hot)
    wide_pad[...] = mm(x_ref[...], one_hot)
    normed_pad[...] = mm(normed, one_hot).astype(BF16)

    @pl.when(section == sections - 1)
    def _():
        upstream[...] = mm(cot_ref[...], one_hot).astype(BF16)

    flat = normed_pad[...].T.reshape(padded // (CORES * PAD), CORES, PAD, tokens)
    even = flat[:, 0].reshape(rail, tokens)
    odd = flat[:, 1].reshape(rail, tokens)
    sides[:, pl.ds(0, tokens)] = jnp.where(core == 0, even, odd)
    sides[:, pl.ds(2 * tokens, tokens)] = jnp.where(core == 0, odd, even)
    other = dp_index(y, x, 1 - core)
    copies.start(
        sides.at[:, pl.ds(2 * tokens, tokens)], sides.at[:, pl.ds(tokens, tokens)], "side", other
    )
    advance(4)
    fetch.wait()
    for start, size in tiles(hidden):
        down_pad[pl.ds(start, size), :] = mm(down_raw[pl.ds(start, size), :], one_hot).astype(BF16)
        advance(2)
    advance(len(steps))
    finish()

    for start, size in tiles(hidden):
        cols = pl.ds(start, size)
        gate = mm(normed_pad[...], weights[:, cols]) * scale_ref[0, 0]
        up = mm(normed_pad[...], weights[:, pl.ds(hidden + start, size)]) * scale_ref[0, 1]
        sigmoid = 1.0 / (1.0 + jnp.exp(-gate))
        slope_gate[:, cols] = up * (sigmoid * (1.0 + gate * (1.0 - sigmoid)))
        slope_up[:, cols] = gate * sigmoid

    def wave_copy(part):
        rows = pl.ds(part * chunk, chunk)
        return pltpu.make_async_remote_copy(
            src_ref=outgoing.at[rows],
            dst_ref=upstream.at[rows],
            send_sem=wave_send.at[part],
            recv_sem=wave_recv.at[part],
            device_id={"section": jnp.maximum(section - 1, 0)},
            device_id_type=pl.DeviceIdType.MESH,
        )

    for part in range(MICRO):
        rows = pl.ds(part * chunk, chunk)

        @pl.when(section < sections - 1)
        def _():
            wave_copy(part).wait_recv()

        above = upstream[rows, :]
        for start, size in tiles(hidden):
            cols = pl.ds(start, size)
            hidden_grad = mm(above, down_pad[cols, :], NT)
            grads[rows, cols] = (hidden_grad * slope_gate[rows, cols]).astype(BF16)
            grads[rows, pl.ds(hidden + start, size)] = (hidden_grad * slope_up[rows, cols]).astype(BF16)
        copies.start(
            grads.at[rows], grads.at[pl.ds(tokens + part * chunk, chunk)], ("grads", part), other
        )
        normed_grad = (
            mm(grads[rows, pl.ds(0, hidden)], weights[:, pl.ds(0, hidden)], NT) * scale_ref[0, 0]
            + mm(grads[rows, pl.ds(hidden, hidden)], weights[:, pl.ds(hidden, hidden)], NT) * scale_ref[0, 1]
        )
        gained = gain_pad[...] * normed_grad
        inverse = inv_ref[rows, :]
        wide = wide_pad[rows, :]
        mean = jnp.sum(wide * gained, axis=-1, keepdims=True) * (1.0 / features)
        outgoing[rows, :] = (
            above.astype(F32) + inverse * gained - wide * (inverse * inverse * inverse) * mean
        ).astype(BF16)

        @pl.when(section > 0)
        def _():
            wave_copy(part).start()

    copies.wait_recv(sides.at[:, pl.ds(tokens, tokens)], "side")
    for part in range(MICRO):
        copies.wait_recv(grads.at[pl.ds(tokens + part * chunk, chunk)], ("grads", part))
    both = sides[:, pl.ds(0, 2 * tokens)]
    for start, size in tiles(2 * hidden):
        cols = pl.ds(start, size)
        rail_ref[:, cols] = mm(both, grads[:, cols]).astype(BF16)
    result_ref[...] = mm(outgoing[...], spread[...], NT).astype(BF16)

    @pl.when(section > 0)
    def _():
        for part in range(MICRO):
            wave_copy(part).wait_send()

    copies.wait_sends()


def adam_update(master, moment_old, second_old, gradient):
    moment_one = beta_one * moment_old + (1.0 - beta_one) * gradient
    moment_two = beta_two * second_old + (1.0 - beta_two) * gradient * gradient
    unbiased_one = moment_one / (1.0 - beta_one**adam_steps)
    unbiased_two = moment_two / (1.0 - beta_two**adam_steps)
    updated = master - learn_rate * (
        unbiased_one / (jnp.sqrt(unbiased_two) + adam_eps) + decay_rate * master
    )
    return (updated, moment_one, moment_two)


def reduce_steps(rail, near, whole, near_last, whole_last, copies, hidden):
    y, x, core = coords()

    def place(half, bulk, other):
        if half == 0:
            return (y + bulk) % RING, (x + other) % RING
        return (y + other) % RING, (x + bulk) % RING

    def block(half, bulk, other, which=None):
        py, px = place(half, bulk, other)
        start, size = {None: (0, PAD), 0: (0, PAD // 2), 1: (PAD // 2, PAD // 2)}[which]
        start = pl.multiple_of((py * RING + px) * PAD + start, PAD // 2)
        return rail.at[pl.ds(start, size), pl.ds(half * hidden, hidden)]

    def send(src, dst, key, half, axis, step):
        py, px = place(half, step, 0) if axis == 0 else place(half, 0, step)
        copies.start(src, dst, key, dp_index(py, px, core))

    def far(half, other):
        for which, step in ((0, 1), (1, -1)):
            send(block(half, 2, other, which), near.at[half, other, which], ("n", half, other, which), half, 0, step)

    def pass_on(half, other):
        for which, step in ((0, 1), (1, -1)):
            copies.wait_recv(near.at[half, other, which], ("n", half, other, which))
            ref = block(half, step, other, which)
            ref[...] = (ref[...].astype(F32) + near[half, other, which].astype(F32)).astype(BF16)
            send(block(half, step, other), whole.at[half, other, which], ("w", half, other, which), half, 0, step)

    def settle(half, other):
        for which in (0, 1):
            copies.wait_recv(whole.at[half, other, which], ("w", half, other, which))
        ref = block(half, 0, other)
        ref[...] = (
            ref[...].astype(F32) + whole[half, other, 0].astype(F32) + whole[half, other, 1].astype(F32)
        ).astype(BF16)

    def far_last(half):
        for which, step in ((0, 1), (1, -1)):
            send(block(half, 0, 2, which), near_last.at[half, which], ("nl", half, which), half, 1, step)

    def pass_last(half):
        for which, step in ((0, 1), (1, -1)):
            copies.wait_recv(near_last.at[half, which], ("nl", half, which))
            ref = block(half, 0, step, which)
            ref[...] = (ref[...].astype(F32) + near_last[half, which].astype(F32)).astype(BF16)
            send(block(half, 0, step), whole_last.at[half, which], ("wl", half, which), half, 1, step)

    def total(half):
        for which in (0, 1):
            copies.wait_recv(whole_last.at[half, which], ("wl", half, which))
        return (
            block(half, 0, 0)[...].astype(F32)
            + whole_last[half, 0].astype(F32)
            + whole_last[half, 1].astype(F32)
        )

    return far, pass_on, settle, far_last, pass_last, total


def update_kernel(
    rail_ref, next_ref, gain_ref, mg_ref, mu_ref, og_ref, ou_ref, sg_ref, su_ref,
    out_ref, nmg_ref, nmu_ref, nog_ref, nou_ref, nsg_ref, nsu_ref, scale_ref,
    weights, rail, near, whole, near_last, whole_last, spread, next_pad, block_ref,
    send_sem, recv_sem, local_sem,
):
    y, x, core = coords()
    hidden = out_ref.shape[1]
    features = next_ref.shape[1]
    copies = Copies(send_sem, recv_sem)
    fetch = pltpu.make_async_copy(rail_ref, rail, local_sem)
    fetch.start()
    plane_barrier()
    fetch.wait()
    far, pass_on, settle, far_last, pass_last, total = reduce_steps(
        rail, near, whole, near_last, whole_last, copies, hidden
    )
    order = (2, 1, 3, 0)
    for other in order:
        far(0, other)
        far(1, other)
    pad_matrix(spread, features)
    widened, inverse = rms(next_ref[...])
    next_normed = (widened * inverse * gain_ref[...]).astype(BF16)
    next_pad[...] = mm(next_normed, spread[...]).astype(BF16)
    for other in order:
        pass_on(0, other)
        pass_on(1, other)
    for other in order:
        settle(0, other)
        settle(1, other)
        if other == 2:
            far_last(0)
            far_last(1)
    pass_last(0)
    pass_last(1)

    begin, steps, finish = gather_steps(weights, copies, hidden)
    mine = pl.multiple_of(lax.axis_index("dp") * PAD, PAD)
    for half, ins, outs in (
        (0, (mg_ref, og_ref, sg_ref), (nmg_ref, nog_ref, nsg_ref)),
        (1, (mu_ref, ou_ref, su_ref), (nmu_ref, nou_ref, nsu_ref)),
    ):
        gradient = total(half)[:ROWS]
        updated, moment, second = adam_update(ins[0][...], ins[1][...], ins[2][...], gradient)
        outs[0][...] = updated
        outs[1][...] = moment
        outs[2][...] = second
        peak = jnp.max(jnp.abs(updated), keepdims=True)
        high = peak.astype(BF16).astype(F32)
        middle = (peak - high).astype(BF16).astype(F32)
        low = peak - high - middle
        tail = lax.broadcasted_iota(jnp.int32, (PAD - ROWS, hidden), 0)
        block_ref[pl.ds(0, ROWS), :] = updated
        block_ref[pl.ds(ROWS, PAD - ROWS), :] = jnp.where(
            tail == 0, high, jnp.where(tail == 1, middle, jnp.where(tail == 2, low, 0.0))
        )
        weights[pl.ds(mine, PAD), pl.ds(half * hidden, hidden)] = block_ref[...].astype(BF16)
        begin(half)
    for step in steps:
        step()
    finish()

    peaks = []
    for half in (0, 1):
        heads = weights[:, pl.ds(half * hidden, 128)].astype(F32)
        heads = heads.reshape(heads.shape[0] // PAD, PAD, 128)[:, PAD - 8 :, :]
        level = lax.broadcasted_iota(jnp.int32, heads.shape, 1)
        found = jnp.sum(jnp.where(level >= 4, heads, 0.0), axis=1)
        peaks.append(jnp.max(found, keepdims=True) + scale_eps)
    lane = lax.broadcasted_iota(jnp.int32, scale_ref.shape, 1)
    scale_ref[...] = jnp.where(lane == 0, peaks[0], peaks[1])
    for start, size in tiles(hidden):
        cols = pl.ds(start, size)
        gate = mm(next_pad[...], weights[:, cols])
        up = mm(next_pad[...], weights[:, pl.ds(hidden + start, size)])
        out_ref[:, cols] = (gate / (1.0 + jnp.exp(-gate)) * up).astype(BF16)
    copies.wait_sends()


VMEM = pl.BlockSpec(memory_space=pltpu.VMEM)
SMEM = pl.BlockSpec(memory_space=pltpu.SMEM)
ANY = pl.BlockSpec(memory_space=pl.ANY)


def shards(
    section_inputs,
    cotangent,
    norm_gain,
    quant_gate,
    quant_up,
    scales,
    down_proj,
    master_gate,
    master_up,
    moment_gate,
    moment_up,
    second_gate,
    second_up,
    next_inputs,
):
    tokens, features = cotangent.shape
    hidden = quant_gate.shape[2]
    partners = lax.axis_size("dp")
    padded = partners * PAD
    rail_rows = padded // CORES
    own = jnp.pad(
        jnp.concatenate([quant_gate[0], quant_up[0]], axis=1), ((0, PAD - ROWS), (0, 0))
    )
    dma = pltpu.SemaphoreType.DMA
    result, rail = pl.pallas_call(
        back_kernel,
        out_shape=(
            jax.ShapeDtypeStruct((tokens, features), BF16),
            jax.ShapeDtypeStruct((rail_rows, 2 * hidden), BF16),
        ),
        in_specs=[VMEM, VMEM, VMEM, VMEM, SMEM, ANY],
        out_specs=(VMEM, VMEM),
        scratch_shapes=[
            pltpu.VMEM((padded, 2 * hidden), BF16),
            pltpu.VMEM((hidden, features), BF16),
            pltpu.VMEM((hidden, padded), BF16),
            pltpu.VMEM((features, padded), BF16),
            pltpu.VMEM((tokens, padded), BF16),
            pltpu.VMEM((tokens, padded), F32),
            pltpu.VMEM((tokens, 1), F32),
            pltpu.VMEM((1, padded), F32),
            pltpu.VMEM((tokens, hidden), F32),
            pltpu.VMEM((tokens, hidden), F32),
            pltpu.VMEM((tokens, padded), BF16),
            pltpu.VMEM((tokens, padded), BF16),
            pltpu.VMEM((2 * tokens, 2 * hidden), BF16),
            pltpu.VMEM((rail_rows, 3 * tokens), BF16),
            dma((80,)),
            dma((80,)),
            dma((MICRO,)),
            dma((MICRO,)),
            dma(()),
        ],
        compiler_params=pltpu.CompilerParams(
            collective_id=0, has_side_effects=True, vmem_limit_bytes=60 * 2**20
        ),
    )(own, section_inputs[0], cotangent, norm_gain, scales, down_proj[0])
    row = jax.ShapeDtypeStruct((ROWS, hidden), F32)
    outs = pl.pallas_call(
        update_kernel,
        out_shape=(jax.ShapeDtypeStruct((tokens, hidden), BF16),)
        + (row,) * 6
        + (jax.ShapeDtypeStruct((1, 2), F32),),
        in_specs=[ANY] + [VMEM] * 8,
        out_specs=(VMEM,) * 8,
        scratch_shapes=[
            pltpu.VMEM((padded, 2 * hidden), BF16),
            pltpu.VMEM((rail_rows, 2 * hidden), BF16),
            pltpu.VMEM((2, RING, 2, PAD // 2, hidden), BF16),
            pltpu.VMEM((2, RING, 2, PAD, hidden), BF16),
            pltpu.VMEM((2, 2, PAD // 2, hidden), BF16),
            pltpu.VMEM((2, 2, PAD, hidden), BF16),
            pltpu.VMEM((features, padded), BF16),
            pltpu.VMEM((tokens, padded), BF16),
            pltpu.VMEM((PAD, hidden), F32),
            dma((128,)),
            dma((128,)),
            dma(()),
        ],
        compiler_params=pltpu.CompilerParams(
            collective_id=1, has_side_effects=True, vmem_limit_bytes=60 * 2**20
        ),
    )(
        rail,
        next_inputs[0],
        norm_gain,
        master_gate[0],
        master_up[0],
        moment_gate[0],
        moment_up[0],
        second_gate[0],
        second_up[0],
    )
    next_hidden, new_gate, new_up, mom_gate, mom_up, sec_gate, sec_up, new_scales = outs
    return (
        result[None],
        new_gate[None],
        new_up[None],
        mom_gate[None],
        mom_up[None],
        sec_gate[None],
        sec_up[None],
        new_scales,
        next_hidden[None],
    )


def solution(mesh):
    placed = (
        P("section", "dp", None),
        P("dp", None),
        P("section", None),
        P("section", "dp", None),
        P("section", "dp", None),
        P("section", None),
        P("section", None, None),
        P("section", "dp", None),
        P("section", "dp", None),
        P("section", "dp", None),
        P("section", "dp", None),
        P("section", "dp", None),
        P("section", "dp", None),
        P("section", "dp", None),
    )
    return jax.shard_map(
        shards,
        mesh=mesh,
        in_specs=placed,
        out_specs=(
            P("section", "dp", None),
            P("section", "dp", None),
            P("section", "dp", None),
            P("section", "dp", None),
            P("section", "dp", None),
            P("section", "dp", None),
            P("section", "dp", None),
            P("section", None),
            P("section", "dp", None),
        ),
        check_vma=False,
    )
```

time: 665 us -> 228 us (0.34)
  waiting for transfers between devices: 380 us -> 0 us
  Pallas kernels: 0 us -> 205 us
  blocking collectives: 157 us -> 0 us
  local copies, waits for them, and re-layouts: 53.1 us -> 19.9 us
  matrix products: 27 us -> 0 us
  starting transfers between devices: 18.3 us -> 0 us
  between operations: 15.9 us -> 0.69 us
  other arithmetic: 11.7 us -> 1.74 us
    pallas_call x0 -> x2, Pallas kernels: none -> 205 us  [the longest x1 136 us: shards(): pl.pallas_call(back_kernel, out_shape=(jax.ShapeDtypeStruct((tokens, feat...]
    ppermute x8 -> x0, waiting for transfers between devices: 204 us -> none  [shifted(): lax.ppermute(value, axis, [(source, source + steps) for source in range(f...]
    all_gather x3 -> x0, waiting for transfers between devices: 162 us -> none  [the longest x1 59.9 us: shards(): lax.all_gather(quant_gate[0], 'dp', axis=0, tiled=True)]
    unnamed x1 -> x0, blocking collectives: 92.3 us -> none
    pmax x1 -> x0, blocking collectives: 64.8 us -> none  [shards(): lax.pmax((jnp.max(jnp.abs(new_gate)), jnp.max(jnp.abs(new_up))), 'dp')]
    dot_general x7 -> x0, matrix products: 27 us -> none  [the longest x1 7.72 us: shards(): lax.dot_general(columns, grads_all, (((0,), (0,)), ((), ())), preferred_e...]
    unnamed x30 -> x18, local copies, waits for them, and re-layouts: 44.2 us -> 19.9 us
    unnamed x7 -> x0, waiting for transfers between devices: 14.3 us -> none
  transfers between devices with their start and end apart: 15 -> 0, of which waited for: 12 -> 0; matrix products, arithmetic and copies ran while one was open for 3% -> 0% of each run, Pallas kernels for 0% -> 0%
where the time goes in v1:
time: 228 us
  Pallas kernels  205 us (90%)
  local copies, waits for them, and re-layouts  19.9 us (9%)
    pallas_call x1, Pallas kernels, shards(): pl.pallas_call(back_kernel, out_shape=(jax.ShapeDtypeStruct((tokens, feat...  136 us
    pallas_call x1, Pallas kernels, shards(): pl.pallas_call(update_kernel, out_shape=(jax.ShapeDtypeStruct((tokens, hi...  69.8 us
    unnamed x18, local copies, waits for them, and re-layouts  19.9 us

profile of v1, /device:TPU:1, one launch (start us, length us, event | category | flops | bytes accessed | tf_op | source)
XLA Modules:
  0.0 227.7 jit_solution(14803215800123707518)
XLA Ops:
  0.6 1.7 fusion.2.own_ref
  2.4 1.9 copy_bitcast_fusion.4
  4.3 1.9 copy_bitcast_fusion.2
  6.2 1.9 copy_bitcast_fusion
  8.1 135.5 %shard_map.205 = (bf16[256,896]{1,0:T(8,128)(2,1)}, bf16[512,4864]{1,0:T(8,128)(2,1)}) custom-call(bf16[32,4864]{1,0:T(8,128)(2,1)} %fusion.2.own_ref, bf16[256,896]{1,0:T(8,128)(2,1)} %bitcast.27, bf16[256,896]{1,0:T(8,128)(2,1)} %cot_ref.1, f32[1,896]{1,0:T(1,128)} %gain_ref.3, f32[1,2]{1,0:T(1,128)} %scale_ref.1, bf16[2432,896]{1,0:T(8,128)(2,1)} %bitcast.25), custom_call_target="tpu_custom_call" | custom-call | tf_op jit(solution)/shard_map/pallas_call | solution.py:513
  143.7 0.0 copy-start.1
  143.7 69.8 %shard_map.206 = (bf16[256,2432]{1,0:T(8,128)(2,1)}, f32[28,2432]{1,0:T(8,128)}, f32[28,2432]{1,0:T(8,128)}, f32[28,2432]{1,0:T(8,128)}, f32[28,2432]{1,0:T(8,12...) custom-call(bf16[512,4864]{1,0:T(8,128)(2,1)} %get-tuple-element.20.rail_ref, ...), custom_call_target="tpu_custom_call" | custom-call | tf_op jit(solution)/shard_map/pallas_call | solution.py:547
  213.5 0.0 copy-start.2
  213.5 0.0 copy-start
  213.5 2.1 copy.23
  215.6 2.0 copy.24
  217.5 2.0 copy.25
  219.5 2.0 copy.26
  221.4 2.0 copy.27
  223.4 2.0 copy.28
  225.3 0.0 copy-done.1
  225.3 0.8 copy.44
  226.1 0.0 copy-done.2
  226.1 0.5 copy.45
  226.6 0.0 copy-done
  226.6 1.0 copy.46
Async XLA Ops:
  143.7 81.7 %copy-start.1 = (bf16[256,896]{1,0:T(8,128)(2,1)S(1)}, bf16[256,896]{1,0:T(8,128)(2,1)}, u32[]{:S(2)}) copy-start(bf16[256,896]{1,0:T(8,128)(2,1)} %get-tuple-element.19) | copy-start | bytes 1376260
  213.5 12.6 %copy-start.2 = (f32[1,2]{1,0:T(1,128)S(1)}, f32[1,2]{1,0:T(1,128)}, u32[]{:S(2)}) copy-start(f32[1,2]{1,0:T(1,128)} %get-tuple-element.60) | copy-start | bytes 28
  213.5 13.1 %copy-start = (bf16[256,2432]{1,0:T(8,128)(2,1)S(1)}, bf16[256,2432]{1,0:T(8,128)(2,1)}, u32[]{:S(2)}) copy-start(bf16[256,2432]{1,0:T(8,128)(2,1)} %get-tuple-element.28) | copy-start | bytes 3735556
